TPU v7x, 32 devices: a whole 2x2x4 slice. The times are simulated.
32 devices in a mesh: chan: 4 (over y, core), lon: 8 (over z, x).
Axes of the slice: x: 2, y: 2, z: 4, core: 2. Of those that a mesh axis runs over, the one named last changes fastest.
Arguments:
- patches: bfloat16 [32, 32, 64, 128], P('chan', None, 'lon'), may hold values from -6 to 6
- embed_weight: bfloat16 [32, 128, 256], P('chan'), may hold values from -0.5 to 0.5
- channel_embed: bfloat16 [32, 256], P('chan'), may hold values from -6 to 6
- agg_query: float32 [256], replicated, may hold values from -160 to 160
- norm_gains: float32 [5, 256], replicated, may hold values from 0.25 to 1.75
- qkv_weight: bfloat16 [2, 256, 768], P(None, None, 'lon'), may hold values from -0.375 to 0.375
- proj_weight: bfloat16 [2, 256, 256], P(None, 'lon'), may hold values from -0.375 to 0.375
- up_weight: bfloat16 [2, 256, 1024], P(None, None, 'lon'), may hold values from -0.375 to 0.375
- down_weight: bfloat16 [2, 1024, 256], P(None, 'lon'), may hold values from -0.1875 to 0.1875
- decode_weight: bfloat16 [32, 256, 128], P('chan'), may hold values from -0.375 to 0.375
Outputs:
- decoded: bfloat16 [32, 32, 64, 128], P('chan', None, 'lon')
All inputs are finite; a program needn't handle non-finite values.
Results may differ from a plain program's by a relative error of at most 0.018.
Values may be sent and summed in bfloat16 or wider, within the bound.
A program may use at most 64 MiB of HBM per device.

v0:
```python
import jax
import jax.numpy as jnp
from jax import lax
from jax.sharding import PartitionSpec as P

HEADS = 8
WC = 8


EPS = 1e-05


def from_behind(value, axis, steps):
    count = lax.axis_size(axis)
    pairs = [(source, (source + steps) % count) for source in range(count)]
    return lax.ppermute(value, axis, pairs)


def as_sent(array):

    def short(part):
        return part.astype(jnp.bfloat16) if part.dtype == jnp.float32 else part

    return jax.tree.map(short, array)


def layer_norm(values, gain):
    mean = jnp.mean(values, axis=-1, keepdims=True)
    centred = values - mean
    spread = jnp.mean(centred * centred, axis=-1, keepdims=True)
    return centred * lax.rsqrt(spread + EPS) * gain


def to_windows(grid):
    rows, cols, width = grid.shape
    count = cols // WC
    return (
        grid.reshape(rows, count, WC, width).transpose(1, 0, 2, 3).reshape(count, rows * WC, width)
    )


def from_windows(windows, rows):
    count, length, width = windows.shape
    return (
        windows.reshape(count, rows, WC, width)
        .transpose(1, 0, 2, 3)
        .reshape(rows, count * WC, width)
    )


def window_block(windows, gain_attn, gain_mlp, weights):
    w_qkv, w_proj, w_up, w_down = weights
    count, length, width = windows.shape
    head_dim = width // HEADS
    flat = windows.reshape(count * length, width)
    normed = layer_norm(flat, gain_attn).astype(jnp.bfloat16)
    qkv = jnp.dot(normed, w_qkv, preferred_element_type=jnp.float32).astype(jnp.bfloat16)
    qkv = qkv.reshape(count, length, 3, HEADS, head_dim)
    scores = jnp.einsum(
        "nqhd,nkhd->nhqk", qkv[:, :, 0], qkv[:, :, 1], preferred_element_type=jnp.float32
    ) * head_dim ** (-0.5)
    probs = jax.nn.softmax(scores, axis=-1).astype(jnp.bfloat16)
    mixed = jnp.einsum(
        "nhqk,nkhd->nqhd", probs, qkv[:, :, 2], preferred_element_type=jnp.float32
    ).astype(jnp.bfloat16)
    mixed = mixed.reshape(count * length, width)
    state = flat + jnp.dot(mixed, w_proj, preferred_element_type=jnp.float32)
    normed = layer_norm(state, gain_mlp).astype(jnp.bfloat16)
    hidden = jax.nn.gelu(jnp.dot(normed, w_up, preferred_element_type=jnp.float32)).astype(
        jnp.bfloat16
    )
    state = state + jnp.dot(hidden, w_down, preferred_element_type=jnp.float32)
    return state.reshape(count, length, width)


def block_weights(layer, qkv_weight, proj_weight, up_weight, down_weight):
    pieces = (qkv_weight[layer], proj_weight[layer], up_weight[layer], down_weight[layer])
    return (
        lax.all_gather(pieces[0], "lon", axis=1, tiled=True),
        lax.all_gather(pieces[1], "lon", axis=0, tiled=True),
        lax.all_gather(pieces[2], "lon", axis=1, tiled=True),
        lax.all_gather(pieces[3], "lon", axis=0, tiled=True),
    )


def body(
    patches,
    embed_weight,
    channel_embed,
    agg_query,
    norm_gains,
    qkv_weight,
    proj_weight,
    up_weight,
    down_weight,
    decode_weight,
):
    chans, rows, cols, width_p = patches.shape
    width = embed_weight.shape[2]
    count = rows * cols
    groups = lax.axis_size("chan")
    owned = count // groups
    own_rows = rows // groups
    flat = patches.reshape(chans, count, width_p)
    embedded = jnp.einsum("ctp,cpe->cte", flat, embed_weight, preferred_element_type=jnp.float32)
    embedded = embedded + channel_embed.astype(jnp.float32)[:, None, :]
    scores = jnp.einsum(
        "cte,e->ct", embedded, agg_query, precision=lax.Precision.HIGHEST
    ) * width ** (-0.5)
    local_top = jnp.max(scores, axis=0)
    shares = jnp.exp(scores - local_top[None])
    numer = jnp.einsum("ct,cte->te", shares, embedded, precision=lax.Precision.HIGHEST)
    denom = jnp.sum(shares, axis=0)
    numer, denom, tops = (
        lax.all_to_all(numer, "chan", split_axis=0, concat_axis=0, tiled=True),
        lax.all_to_all(denom, "chan", split_axis=0, concat_axis=0, tiled=True),
        lax.all_to_all(local_top, "chan", split_axis=0, concat_axis=0, tiled=True),
    )
    numer = numer.reshape(groups, owned, width)
    denom = denom.reshape(groups, owned)
    tops = tops.reshape(groups, owned)
    best = jnp.max(tops, axis=0)
    factor = jnp.exp(tops - best[None])
    numer = jnp.sum(factor[:, :, None] * numer, axis=0)
    denom = jnp.sum(factor * denom, axis=0)
    state = (numer / denom[:, None]).reshape(own_rows, cols, width)
    weights = block_weights(0, qkv_weight, proj_weight, up_weight, down_weight)
    state = from_windows(
        window_block(to_windows(state), norm_gains[0], norm_gains[1], weights), own_rows
    )
    half = WC // 2
    edge = from_behind(state[:, :half].astype(jnp.bfloat16), "lon", -1).astype(jnp.float32)
    moved = jnp.concatenate([state[:, half:], edge], axis=1)
    weights = block_weights(1, qkv_weight, proj_weight, up_weight, down_weight)
    moved = from_windows(
        window_block(to_windows(moved), norm_gains[2], norm_gains[3], weights), own_rows
    )
    back = from_behind(as_sent(moved[:, cols - half :]), "lon", 1)
    state = jnp.concatenate([back, moved[:, : cols - half]], axis=1)
    final = layer_norm(state.reshape(owned, width), norm_gains[4]).astype(jnp.bfloat16)
    decoded = jnp.einsum(
        "te,cep->ctp",
        lax.all_gather(final, "chan", axis=0, tiled=True),
        decode_weight,
        preferred_element_type=jnp.float32,
    ).astype(jnp.bfloat16)
    return decoded.reshape(chans, rows, cols, width_p)


def solution(mesh):
    placed = (
        P("chan", None, "lon", None),
        P("chan", None, None),
        P("chan", None),
        P(),
        P(),
        P(None, None, "lon"),
        P(None, "lon", None),
        P(None, None, "lon"),
        P(None, "lon", None),
        P("chan", None, None),
    )
    return jax.shard_map(
        body, mesh=mesh, in_specs=placed, out_specs=P("chan", None, "lon", None), check_vma=False
    )
```

profile of v0, /device:TPU:0, one launch (start us, length us, event | category | flops | bytes accessed | tf_op | source)
XLA Modules:
  0.0 300.7 jit_solution(9474477746949783212)
XLA Ops:
  0.0 0.7 convert_element_type.70
  0.8 0.3 copy-done
  1.1 1.5 convolution_add_fusion
  2.6 1.9 fusion.112
  4.4 0.7 all_to_all.18
  5.1 4.3 %all-to-all-start = ((f32[4,64,1]{1,2,0:T(1,128)}), f32[4,64,1]{1,2,0:T(1,128)}, u32[]{:S(2)}, u32[]{:S(2)}) async-start(f32[4,64,1]{1,2,0:T(1,128)} %bitcast.3), calls=%async_computation | async-start | bytes 4096 | tf_op jit(solution)/shard_map/all_to_all | solution.py:117
  9.4 0.6 fusion.86
  10.1 3.0 fusion.2
  13.1 0.6 fusion.107
  13.8 34.3 %all-gather = bf16[1,256,768]{1,2,0:T(8,128)(2,1)} all-gather(bf16[1,256,96]{1,2,0:T(8,128)(2,1)S(1)} %get-tuple-element.9), channel_id=2, replica_groups=mesh['chan'=4,'lon'=8] {'lon'}, dimensions={2}, use_global_device_ids=true | all-gather | bytes 442368 | tf_op jit(solution)/shard_map/all_gather | solution.py:79
  48.1 27.1 %all-gather.2 = bf16[1,256,1024]{2,1,0:T(8,128)(2,1)S(1)} all-gather(bf16[1,256,128]{2,1,0:T(8,128)(2,1)S(1)} %get-tuple-element.6), channel_id=4, replica_groups=mesh['chan'=4,'lon'=8] {'lon'}, dimensions={2}, use_global_device_ids=true | all-gather | bytes 589824 | tf_op jit(solution)/shard_map/all_gather | solution.py:81
  75.1 33.5 %all-gather.3 = bf16[1,1024,256]{2,1,0:T(8,128)(2,1)} all-gather(bf16[1,128,256]{2,1,0:T(8,128)(2,1)S(1)} %get-tuple-element.8), channel_id=5, replica_groups=mesh['chan'=4,'lon'=8] {'lon'}, dimensions={1}, use_global_device_ids=true | all-gather | bytes 589824 | tf_op jit(solution)/shard_map/all_gather | solution.py:82
  108.7 28.1 %all-gather.6 = bf16[1,256,1024]{2,1,0:T(8,128)(2,1)S(1)} all-gather(bf16[1,256,128]{2,1,0:T(8,128)(2,1)S(1)} %get-tuple-element.5), channel_id=8, replica_groups=mesh['chan'=4,'lon'=8] {'lon'}, dimensions={2}, use_global_device_ids=true | all-gather | bytes 589824 | tf_op jit(solution)/shard_map/all_gather | solution.py:81
  136.7 31.4 %all-gather.7 = bf16[1,1024,256]{2,1,0:T(8,128)(2,1)S(1)} all-gather(bf16[1,128,256]{2,1,0:T(8,128)(2,1)S(1)} %get-tuple-element.7), channel_id=9, replica_groups=mesh['chan'=4,'lon'=8] {'lon'}, dimensions={1}, use_global_device_ids=true | all-gather | bytes 589824 | tf_op jit(solution)/shard_map/all_gather | solution.py:82
  168.1 30.9 %all-gather.4 = bf16[1,256,768]{1,2,0:T(8,128)(2,1)S(1)} all-gather(bf16[1,256,96]{1,2,0:T(8,128)(2,1)S(1)} %get-tuple-element.10), channel_id=6, replica_groups=mesh['chan'=4,'lon'=8] {'lon'}, dimensions={2}, use_global_device_ids=true | all-gather | bytes 442368 | tf_op jit(solution)/shard_map/all_gather | solution.py:79
  199.1 0.7 all_to_all.22
  199.8 3.2 %all-to-all-start.2 = ((f32[4,64,1]{1,2,0:T(1,128)}), f32[4,64,1]{1,2,0:T(1,128)S(1)}, u32[]{:S(2)}, u32[]{:S(2)}) async-start(f32[4,64,1]{1,2,0:T(1,128)} %all_to_all.22), calls=%async_computation.2 | async-start | bytes 4096 | tf_op jit(solution)/shard_map/all_to_all | solution.py:116
  203.0 30.5 %all-gather.1 = bf16[1,256,256]{2,1,0:T(8,128)(2,1)S(1)} all-gather(bf16[1,32,256]{2,1,0:T(8,128)(2,1)S(1)} %get-tuple-element.12), channel_id=3, replica_groups=mesh['chan'=4,'lon'=8] {'lon'}, dimensions={1}, use_global_device_ids=true | all-gather | bytes 147456 | tf_op jit(solution)/shard_map/all_gather | solution.py:80
  233.5 0.7 copy.36
  234.2 0.7 reduce_max.37
  234.9 3.6 %all-to-all-start.1 = ((f32[4,64,256]{2,1,0:T(8,128)}), f32[4,64,256]{2,1,0:T(8,128)S(1)}, u32[]{:S(2)}, u32[]{:S(2)}) async-start(f32[4,64,256]{2,1,0:T(8,128)} %bitcast.7), calls=%async_computation.1 | async-start | bytes 524288 | tf_op jit(solution)/shard_map/all_to_all | solution.py:115
  238.5 0.7 multiply_reduce_fusion.6
  239.2 0.7 subtract_exponential_fusion.1
  239.9 4.6 %all-to-all-done.1 = f32[4,64,256]{2,1,0:T(8,128)S(1)} async-done(((f32[4,64,256]{2,1,0:T(8,128)}), f32[4,64,256]{2,1,0:T(8,128)S(1)}, u32[]{:S(2)}, u32[]{:S(2)}) %all-to-all-start.1) | async-done | bytes 262176 | tf_op jit(solution)/shard_map/all_to_all | solution.py:115
  244.6 0.2 fusion.102
  244.8 0.2 multiply_reduce_fusion.5
  245.0 1.9 convolution_convert_fusion.2
  246.9 1.1 copy.29
  248.0 0.9 convolution_multiply_fusion.1
  248.9 0.3 fusion.108
  249.2 1.2 convolution_convert_fusion.4
  250.4 0.9 fusion.109
  251.4 0.2 multiply_reduce_fusion.4
  251.6 1.1 fusion.10
  252.8 0.6 collective-permute-start
  253.3 30.6 %all-gather.5 = bf16[1,256,256]{2,1,0:T(8,128)(2,1)S(1)} all-gather(bf16[1,32,256]{2,1,0:T(8,128)(2,1)S(1)} %get-tuple-element.11), channel_id=7, replica_groups=mesh['chan'=4,'lon'=8] {'lon'}, dimensions={1}, use_global_device_ids=true | all-gather | bytes 147456 | tf_op jit(solution)/shard_map/all_gather | solution.py:80
  284.0 0.2 multiply_reduce_fusion.3
  284.4 0.9 convolution_convert_fusion.1
  285.3 0.2 copy.31
  285.5 0.2 convolution_multiply_fusion
  285.7 0.3 fusion.110
  286.0 0.2 convolution_convert_fusion.3
  286.2 0.3 fusion.111
  286.5 0.2 multiply_reduce_fusion.2
  286.7 0.5 fusion.9
  287.3 6.4 %collective-permute-done.1 = bf16[8,4,256]{2,1,0:T(4,128)(2,1)S(1)} collective-permute-done((bf16[8,4,256]{2,1,0:T(4,128)(2,1)S(1)}, bf16[8,4,256]{2,1,0:T(4,128)(2,1)S(1)}, u32[]{:S(2)}, u32[]{:S(2)}) %collective-permute-start.1) | collective-permute-done | bytes 16416 | tf_op jit(solution)/shard_map/ppermute | solution.py:16
  294.2 5.4 %all_gather.35 = bf16[256,256]{1,0:T(8,128)(2,1)S(1)} all-gather(bf16[64,256]{1,0:T(8,128)(2,1)S(1)} %fusion.61), channel_id=1, replica_groups=mesh['chan'=4,'lon'=8] {'chan'}, dimensions={0}, use_global_device_ids=true | all-gather | bytes 163840 | tf_op jit(solution)/shard_map/all_gather | solution.py:143
  299.6 1.1 fusion.4
  (60 shorter events, 1.3 us)
Async XLA Ops:
  0.0 1.1 copy-start
  0.0 2.5 copy-start.11
  2.5 10.6 %copy-start.10 = (f32[5,256]{1,0:T(8,128)S(1)}, f32[5,256]{1,0:T(8,128)}, u32[]{:S(2)}) copy-start(f32[5,256]{1,0:T(8,128)} %param.14) | copy-start | bytes 15364
  2.5 11.2 %copy-start.5 = (bf16[2,256,96]{1,2,0:T(8,128)(2,1)S(1)}, bf16[2,256,96]{1,2,0:T(8,128)(2,1)}, u32[]{:S(2)}) copy-start(bf16[2,256,96]{1,2,0:T(8,128)(2,1)} %param.15) | copy-start | bytes 294916
  4.4 43.6 %copy-start.6 = (bf16[2,32,256]{2,1,0:T(8,128)(2,1)S(1)}, bf16[2,32,256]{2,1,0:T(8,128)(2,1)}, u32[]{:S(2)}) copy-start(bf16[2,32,256]{2,1,0:T(8,128)(2,1)} %param.16) | copy-start | bytes 98308
  4.4 43.6 %copy-start.3 = (bf16[2,256,128]{2,1,0:T(8,128)(2,1)S(1)}, bf16[2,256,128]{2,1,0:T(8,128)(2,1)}, u32[]{:S(2)}) copy-start(bf16[2,256,128]{2,1,0:T(8,128)(2,1)} %param.17) | copy-start | bytes 393220
  5.1 194.7 %all-to-all-start = ((f32[4,64,1]{1,2,0:T(1,128)}), f32[4,64,1]{1,2,0:T(1,128)}, u32[]{:S(2)}, u32[]{:S(2)}) async-start(f32[4,64,1]{1,2,0:T(1,128)} %bitcast.3), calls=%async_computation | async-start | bytes 4096 | tf_op jit(solution)/shard_map/all_to_all | solution.py:117
  10.0 65.1 %copy-start.4 = (bf16[2,128,256]{2,1,0:T(8,128)(2,1)S(1)}, bf16[2,128,256]{2,1,0:T(8,128)(2,1)}, u32[]{:S(2)}) copy-start(bf16[2,128,256]{2,1,0:T(8,128)(2,1)} %param.18) | copy-start | bytes 393220
  13.1 186.0 %copy-start.9 = (f32[256]{0:T(256)S(1)}, f32[256]{0:T(256)}, u32[]{:S(2)}) copy-start(f32[256]{0:T(256)} %get-tuple-element.13) | copy-start | bytes 3076
  199.8 35.2 %all-to-all-start.2 = ((f32[4,64,1]{1,2,0:T(1,128)}), f32[4,64,1]{1,2,0:T(1,128)S(1)}, u32[]{:S(2)}, u32[]{:S(2)}) async-start(f32[4,64,1]{1,2,0:T(1,128)} %all_to_all.22), calls=%async_computation.2 | async-start | bytes 4096 | tf_op jit(solution)/shard_map/all_to_all | solution.py:116
  234.9 16.7 %copy-start.1 = (bf16[1,1024,256]{2,1,0:T(8,128)(2,1)S(1)}, bf16[1,1024,256]{2,1,0:T(8,128)(2,1)}, u32[]{:S(2)}) copy-start(bf16[1,1024,256]{2,1,0:T(8,128)(2,1)} %all-gather.3) | copy-start | bytes 1572868
  234.9 9.5 %all-to-all-start.1 = ((f32[4,64,256]{2,1,0:T(8,128)}), f32[4,64,256]{2,1,0:T(8,128)S(1)}, u32[]{:S(2)}, u32[]{:S(2)}) async-start(f32[4,64,256]{2,1,0:T(8,128)} %bitcast.7), calls=%async_computation.1 | async-start | bytes 524288 | tf_op jit(solution)/shard_map/all_to_all | solution.py:115
  239.2 11.2 %copy-start.7 = (f32[64]{0:T(128)}, f32[64]{0:T(128)S(1)}, u32[]{:S(2)}) copy-start(f32[64]{0:T(128)S(1)} %multiply_reduce_fusion.6) | copy-start | bytes 772
  252.7 33.9 %copy-start.12 = (f32[1,256]{1,0:T(1,128)S(1)}, f32[1,256]{1,0:T(1,128)}, u32[]{:S(2)}) copy-start(f32[1,256]{1,0:T(1,128)} %get-tuple-element.19) | copy-start | bytes 3076
  252.8 31.1 %collective-permute-start = (bf16[8,4,256]{2,1,0:T(4,128)(2,1)S(1)}, bf16[8,4,256]{2,1,0:T(4,128)(2,1)S(1)}, u32[]{:S(2)}, u32[]{:S(2)}) collective-permute-start(bf16[8,4,256]{2,1,0:T(4,128)(2,1)S(1)} %slice.127), channel_id=1, source_target_pairs={{0,7},{1,0},{2,1},{3,2},{4,3},{5,4},{6,5},{7,6},{8,15},{9,8},{10,9... | collective-permute-start | bytes 49160 | tf_op jit(solution)/shard_map/ppermute | solution.py:16
  285.4 8.7 %copy-start.8 = (f32[1,256]{1,0:T(1,128)S(1)}, f32[1,256]{1,0:T(1,128)}, u32[]{:S(2)}) copy-start(f32[1,256]{1,0:T(1,128)} %get-tuple-element.15) | copy-start | bytes 3076
  285.7 13.9 %copy-start.2 = (bf16[8,256,128]{2,1,0:T(8,128)(2,1)S(1)}, bf16[8,256,128]{2,1,0:T(8,128)(2,1)}, u32[]{:S(2)}) copy-start(bf16[8,256,128]{2,1,0:T(8,128)(2,1)} %param.19) | copy-start | bytes 1572868
  287.2 6.5 %collective-permute-start.1 = (bf16[8,4,256]{2,1,0:T(4,128)(2,1)S(1)}, bf16[8,4,256]{2,1,0:T(4,128)(2,1)S(1)}, u32[]{:S(2)}, u32[]{:S(2)}) collective-permute-start(bf16[8,4,256]{2,1,0:T(4,128)(2,1)S(1)} %slice.126), channel_id=1, source_target_pairs={{0,1},{1,2},{2,3},{3,4},{4,5},{5,6},{6,7},{7,0},{8,9},{9,10},{10,1... | collective-permute-start | bytes 49160 | tf_op jit(solution)/shard_map/ppermute | solution.py:16
where the time goes:
time: 301 us
  blocking collectives  252 us (84%)
  matrix products  16.2 us (5%)
  starting transfers between devices  11.7 us (4%)
  waiting for transfers between devices  11 us (4%)
  other arithmetic  4.94 us (2%)
  local copies, waits for them, and re-layouts  4.76 us (2%)
    all_gather x2, blocking collectives, block_weights(): lax.all_gather(pieces[0], 'lon', axis=1, tiled=True)  65.2 us
    all_gather x2, blocking collectives, block_weights(): lax.all_gather(pieces[3], 'lon', axis=0, tiled=True)  64.9 us
    all_gather x2, blocking collectives, block_weights(): lax.all_gather(pieces[1], 'lon', axis=0, tiled=True)  61.1 us
    all_gather x2, blocking collectives, block_weights(): lax.all_gather(pieces[2], 'lon', axis=1, tiled=True)  55.1 us
    ppermute x2, waiting for transfers between devices, from_behind(): return lax.ppermute(value, axis, pairs)  6.41 us
  transfers between devices with their start and end apart: 5, of which 2 were waited for; matrix products, arithmetic and copies ran while one was open for 2% of the time, Pallas kernels for 0%

commit v1 on v0

v1 whole, which is shorter than its diff:
```python
import functools

import jax
import jax.numpy as jnp
from jax import lax
from jax.experimental import pallas as pl
from jax.experimental.pallas import tpu as pltpu
from jax.sharding import PartitionSpec as P

HEADS = 8
WC = 8
EPS = 1e-05
MESH = pl.DeviceIdType.MESH
BF16 = jnp.bfloat16
F32 = jnp.float32
NT = (((1,), (1,)), ((), ()))


def layer_norm(values, gain):
    mean = jnp.mean(values, axis=-1, keepdims=True)
    centred = values - mean
    spread = jnp.mean(centred * centred, axis=-1, keepdims=True)
    return centred * lax.rsqrt(spread + EPS) * gain


def merged(block):
    shards, rows, width = block.shape
    if rows % 16:
        return block.astype(F32).reshape(shards * rows, width).astype(BF16)
    return block.reshape(shards * rows, width)


def inner_factor(count):
    inner = 1
    while inner * inner * 4 <= count:
        inner *= 2
    return inner if count % inner == 0 else 1


class Sems:
    def __init__(self, ref=None):
        self.ref, self.used = ref, 0

    def take(self):
        self.used += 1
        return None if self.ref is None else self.ref.at[self.used - 1]


class Gather:
    def __init__(self, buf, geometry, x_first, sends, recvs):
        self.buf = buf
        self.geometry, self.x_first = geometry, x_first
        self.sends, self.recvs = sends, recvs
        self.pending = []
        self.late = []

    def rows(self, core):
        half = self.buf.shape[1] // 2
        return pl.ds(pl.multiple_of(core * half, half), half)

    def copy(self, first, count, core, target, sem_pair):
        piece = self.buf.at[pl.ds(first, count), self.rows(core)]
        return pltpu.make_async_remote_copy(
            src_ref=piece,
            dst_ref=piece,
            send_sem=sem_pair[0],
            recv_sem=sem_pair[1],
            device_id=target,
            device_id_type=MESH,
        )

    def pair(self):
        return self.sends.take(), self.recvs.take()

    def begin(self, copy, when=None):
        if when is None:
            copy.start()
        else:
            pl.when(when)(copy.start)
        self.pending.append((copy, when))

    def arrive(self, copy, when=None):
        if when is None:
            copy.wait_recv()
        else:
            pl.when(when)(copy.wait_recv)

    def share(self, first, count, when=None):
        g = self.geometry
        pair = self.pair()
        self.begin(self.copy(first, count, g["core"], g["partner"], pair), when)
        self.late.append((self.copy(first, count, 1 - g["core"], g["partner"], pair), when))

    def across(self, z, when=None):
        g = self.geometry
        inner, x, core = g["inner"], g["x"], g["core"]
        incoming = []
        for step in range(1, inner):
            pair = self.pair()
            to, source = lax.rem(x + step, inner), lax.rem(x + inner - step, inner)
            peer = g["at"](g["z"], to)
            self.begin(self.copy(z * inner + x, 1, core, peer, pair), when)
            incoming.append((z * inner + source, self.copy(z * inner + source, 1, core, peer, pair), when))
        return incoming

    def steps(self):
        g = self.geometry
        inner, outer, x, z, core = g["inner"], g["outer"], g["x"], g["z"], g["core"]
        width = inner if self.x_first else 1

        def first_of(at):
            return at * inner if self.x_first else at * inner + x

        if self.x_first:
            incoming = self.across(z)
            yield
            for _, copy, when in incoming:
                self.arrive(copy, when)
            for shard, _, when in incoming:
                self.share(shard, 1, when)
        crossing = []
        for step in range(outer):
            if step < outer - 1:
                right, left = self.pair(), self.pair()
                here_right = (z + 1 < outer) & (z - step >= 0)
                here_left = (z - 1 >= 0) & (z + step < outer)
                at_right, at_left = jnp.maximum(z - step, 0), jnp.minimum(z + step, outer - 1)
                up, down = jnp.minimum(z + 1, outer - 1), jnp.maximum(z - 1, 0)
                self.begin(self.copy(first_of(at_right), width, core, g["at"](up, x), right), here_right)
                self.begin(self.copy(first_of(at_left), width, core, g["at"](down, x), left), here_left)
            if step == 0:
                arrived = [(z, None)]
            for at, when in arrived:
                if not self.x_first:
                    crossing += self.across(at, when)
                if step:
                    self.share(first_of(at), width, when)
            if step == outer - 1:
                break
            yield
            from_left, from_right = z - 1 - step >= 0, z + 1 + step < outer
            at_left, at_right = jnp.maximum(z - 1 - step, 0), jnp.minimum(z + 1 + step, outer - 1)
            self.arrive(self.copy(first_of(at_left), width, core, g["at"](down, x), right), from_left)
            self.arrive(self.copy(first_of(at_right), width, core, g["at"](up, x), left), from_right)
            arrived = [(at_left, from_left), (at_right, from_right)]
        for shard, copy, when in crossing:
            yield
            self.arrive(copy, when)
            self.share(shard, 1, when)
        yield
        for copy, when in self.late:
            self.arrive(copy, when)

    def finish(self):
        for copy, when in self.pending:
            if when is None:
                copy.wait_send()
            else:
                pl.when(when)(copy.wait_send)


def window_block(state, gain_attn, gain_mlp, attn_ref, mlp_ref, sizes):
    n_qkv, n_up = sizes
    length, width = state.shape
    head_dim = width // HEADS
    normed = layer_norm(state, gain_attn).astype(BF16)
    w_qkv = merged(attn_ref[:, :n_qkv])
    qkv = lax.dot_general(normed, w_qkv, NT, preferred_element_type=F32).astype(BF16)
    query, key, value = (qkv[:, i * width : (i + 1) * width] for i in range(3))
    head = lax.broadcasted_iota(jnp.int32, (length, width), 1) // head_dim
    zero = jnp.zeros((), F32)
    wide = query.astype(F32)
    stacked = jnp.concatenate(
        [jnp.where(head == h, wide, zero).astype(BF16) for h in range(HEADS)], axis=0
    )
    scores = lax.dot_general(stacked, key, NT, preferred_element_type=F32) * head_dim ** (-0.5)
    scores = jnp.exp(scores - jnp.max(scores, axis=-1, keepdims=True))
    probs = (scores / jnp.sum(scores, axis=-1, keepdims=True)).astype(BF16)
    every = jnp.dot(probs, value, preferred_element_type=F32)
    mixed = jnp.zeros((length, width), F32)
    for h in range(HEADS):
        mixed = jnp.where(head == h, every[h * length : (h + 1) * length], mixed)
    w_proj = merged(attn_ref[:, n_qkv:])
    state = state + jnp.dot(mixed.astype(BF16), w_proj, preferred_element_type=F32)
    normed = layer_norm(state, gain_mlp).astype(BF16)
    w_up = merged(mlp_ref[:, :n_up])
    hidden = lax.dot_general(normed, w_up, NT, preferred_element_type=F32)
    hidden = jax.nn.gelu(hidden).astype(BF16)
    w_down = merged(mlp_ref[:, n_up:])
    return state + jnp.dot(hidden, w_down, preferred_element_type=F32)


def sem_count(outer, inner, x_first):
    moves = 2 * (outer - 1)
    if x_first:
        return 2 * (inner - 1) + 2 * moves
    return 2 * moves + (1 + moves) * (inner - 1) * 2


def kernel(
    groups, lons, inner, sizes,
    patches, embed_weight, channel_embed, agg_query, gains, packed, decode_weight,
    out,
    embedded, partial, aux_out, aux_in, mean_in, attn0, mlp0, attn1, mlp1, edge_out, edge_in, final_out, final_in,
    chunk_send, chunk_recv, own_sem, agg_send, agg_recv, aux_send, aux_recv, edge_send, edge_recv, fin_send, fin_recv,
):
    chans, count, _ = patches.shape
    width = embed_weight.shape[2]
    owned = count // groups
    half = owned // 2
    me, lon = lax.axis_index("chan"), lax.axis_index("lon")
    west, east = lax.rem(lon + lons - 1, lons), lax.rem(lon + 1, lons)
    barrier = pltpu.get_barrier_semaphore()
    greeted = 0
    for step in range(1, lons):
        pl.semaphore_signal(barrier, inc=1, device_id=(me, lax.rem(lon + step, lons)), device_id_type=MESH)
        greeted += 1
    for step in range(1, groups):
        other = lax.rem(me + step, groups)
        for column in (lon, west, east):
            pl.semaphore_signal(barrier, inc=1, device_id=(other, column), device_id_type=MESH)
            greeted += 1

    n_qkv, n_proj, n_up, n_down = sizes
    n_attn = n_qkv + n_proj
    core = lax.rem(me, 2)
    outer = lons // inner
    geometry = {
        "inner": inner, "outer": outer, "core": core,
        "x": lax.rem(lon, inner), "z": lon // inner,
        "partner": (me + 1 - 2 * core, lon),
        "at": lambda z, x: (me, z * inner + x),
    }
    bufs = (attn0, mlp0, attn1, mlp1)
    own_copies = []
    for at, buf in enumerate(bufs):
        layer, rows = at // 2, pl.ds(0, n_attn) if at % 2 == 0 else pl.ds(n_attn, n_up + n_down)
        copy = pltpu.make_async_copy(packed.at[layer, rows], buf.at[lon], own_sem.at[at])
        copy.start()
        own_copies.append(copy)

    query = agg_query[...]
    scores = []
    for c in range(chans):
        value = jnp.dot(patches[c], embed_weight[c], preferred_element_type=F32)
        value = value + channel_embed[c : c + 1].astype(F32)
        embedded[c] = value
        scores.append(jnp.sum(value * query, axis=-1, keepdims=True) * width ** (-0.5))

    for copy in own_copies:
        copy.wait()
    pl.semaphore_wait(barrier, greeted)

    offset, gathers = 0, []
    for at, order in enumerate((True, False, False, True)):
        pairs = sem_count(outer, inner, order)
        sends, recvs = Sems(chunk_send.at[pl.ds(offset, pairs)]), Sems(chunk_recv.at[pl.ds(offset, pairs)])
        gathers.append(Gather(bufs[at], geometry, order, sends, recvs))
        offset += pairs
    flows = [one.steps() for one in gathers]
    for flow in flows:
        next(flow)

    top = functools.reduce(jnp.maximum, scores)
    shares = [jnp.exp(score - top) for score in scores]
    denom = functools.reduce(jnp.add, shares)
    lane = lax.broadcasted_iota(jnp.int32, (count, 128), 1)
    aux = jnp.where(lane == 0, top, jnp.where(lane == 1, denom, 0.0))
    numer = shares[0] * embedded[0]
    for c in range(1, chans):
        numer = numer + shares[c] * embedded[c]
    mean = numer / denom
    for g in range(groups):
        partial[g] = mean[g * owned : (g + 1) * owned].astype(BF16)
        block = aux[g * owned : (g + 1) * owned]
        if owned < 128:
            block = jnp.concatenate([block, jnp.zeros((128 - owned, 128), F32)], axis=0)
        aux_out[g] = block.T[:8]
    sent = []
    for step in range(1, groups):
        to = lax.rem(me + step, groups)
        sent.append(
            pltpu.make_async_remote_copy(
                src_ref=partial.at[to], dst_ref=mean_in.at[step - 1],
                send_sem=agg_send.at[step - 1], recv_sem=agg_recv.at[step - 1],
                device_id=(to, lon), device_id_type=MESH,
            )
        )
        sent.append(
            pltpu.make_async_remote_copy(
                src_ref=aux_out.at[to], dst_ref=aux_in.at[step - 1],
                send_sem=aux_send.at[step - 1], recv_sem=aux_recv.at[step - 1],
                device_id=(to, lon), device_id_type=MESH,
            )
        )
    for copy in sent:
        copy.start()

    def drain(*which):
        live = [flows[i] for i in which]
        while live:
            for flow in list(live):
                if next(flow, "end") == "end":
                    live.remove(flow)

    drain(0, 1)

    for copy in sent:
        copy.wait_recv()
    means = [partial[me].astype(F32)] + [mean_in[i].astype(F32) for i in range(groups - 1)]
    columns = [aux_out[me].T] + [aux_in[i].T for i in range(groups - 1)]
    tops = [column[:owned, 0:1] for column in columns]
    best = functools.reduce(jnp.maximum, tops)
    weights = [column[:owned, 1:2] * jnp.exp(one - best) for column, one in zip(columns, tops)]
    total = functools.reduce(jnp.add, weights)
    state = functools.reduce(jnp.add, [w * m for w, m in zip(weights, means)]) / total

    side = WC // 2

    def order_matrix(flip, kind):
        row = lax.broadcasted_iota(jnp.int32, (owned, owned), 1 if flip else 0)
        token = lax.broadcasted_iota(jnp.int32, (owned, owned), 0 if flip else 1)
        within = row % half
        return jnp.where((within // side) * WC + (row // half) * side + within % side == token, 1.0, 0.0).astype(kind)

    state = jnp.dot(order_matrix(False, F32), state, precision=lax.Precision.HIGHEST, preferred_element_type=F32)

    def gain(i):
        return gains[i : i + 1]

    state = window_block(state, gain(0), gain(1), attn0, mlp0, (n_qkv, n_up))
    edge_out[...] = state[:half].astype(BF16)
    edge = pltpu.make_async_remote_copy(
        src_ref=edge_out, dst_ref=edge_in, send_sem=edge_send.at[0], recv_sem=edge_recv.at[0],
        device_id=(me, west), device_id_type=MESH,
    )
    edge.start()
    drain(2, 3)
    edge.wait_recv()
    moved = jnp.concatenate([state[half:], edge_in[...].astype(F32)], axis=0)
    moved = window_block(moved, gain(2), gain(3), attn1, mlp1, (n_qkv, n_up))
    final = layer_norm(moved, gain(4)).astype(BF16)
    final_out[0] = final[half:]
    final_out[1] = final[:half]
    last = []
    for step in range(groups):
        to = lax.rem(me + step, groups)
        last.append(
            pltpu.make_async_remote_copy(
                src_ref=final_out.at[0], dst_ref=final_in.at[me, 0],
                send_sem=fin_send.at[step, 0], recv_sem=fin_recv.at[step, 0],
                device_id=(to, east), device_id_type=MESH,
            )
        )
        if step:
            last.append(
                pltpu.make_async_remote_copy(
                    src_ref=final_out.at[1], dst_ref=final_in.at[me, 1],
                    send_sem=fin_send.at[step, 1], recv_sem=fin_recv.at[step, 1],
                    device_id=(to, lon), device_id_type=MESH,
                )
            )
    for copy in last:
        copy.start()
    final_in[me, 1] = final[:half]
    arrivals = []
    for step in range(groups):
        source = lax.rem(me + groups - step, groups)
        for part in range(2):
            if step or part == 0:
                pltpu.make_async_remote_copy(
                    src_ref=final_out.at[part], dst_ref=final_in.at[source, part],
                    send_sem=fin_send.at[step, part], recv_sem=fin_recv.at[step, part],
                    device_id=(source, west if part == 0 else lon) if step else (me, west), device_id_type=MESH,
                ).wait_recv()
    back = order_matrix(True, BF16)
    tokens = []
    for g in range(groups):
        both = merged(final_in[g])
        tokens.append(jnp.dot(back, both, preferred_element_type=F32).astype(BF16))
    tokens = jnp.concatenate(tokens, axis=0)
    for c in range(chans):
        out[c] = jnp.dot(tokens, decode_weight[c], preferred_element_type=F32).astype(BF16)

    for one in gathers:
        one.finish()
    for copy in sent + [edge] + last:
        copy.wait_send()


def body(
    patches, embed_weight, channel_embed, agg_query, norm_gains,
    qkv_weight, proj_weight, up_weight, down_weight, decode_weight,
):
    chans, rows, cols, width_p = patches.shape
    width = embed_weight.shape[2]
    count = rows * cols
    groups, lons = lax.axis_size("chan"), lax.axis_size("lon")
    owned = count // groups
    half = owned // 2
    assert cols == WC and owned <= 128
    packed = jnp.concatenate(
        [qkv_weight.transpose(0, 2, 1), proj_weight, up_weight.transpose(0, 2, 1), down_weight], axis=1
    )
    sizes = (qkv_weight.shape[2], proj_weight.shape[1], up_weight.shape[2], down_weight.shape[1])
    n_attn, n_mlp = sizes[0] + sizes[1], sizes[2] + sizes[3]
    inner = inner_factor(lons)
    outer = lons // inner
    pairs = sum(sem_count(outer, inner, order) for order in (True, False, False, True))
    vmem = pl.BlockSpec(memory_space=pltpu.VMEM)
    out = pl.pallas_call(
        functools.partial(kernel, groups, lons, inner, sizes),
        out_shape=jax.ShapeDtypeStruct((chans, count, decode_weight.shape[2]), BF16),
        in_specs=[vmem] * 7,
        out_specs=vmem,
        scratch_shapes=[
            pltpu.VMEM((chans, count, width), F32),
            pltpu.VMEM((groups, owned, width), BF16),
            pltpu.VMEM((groups, 8, 128), F32),
            pltpu.VMEM((groups - 1, 8, 128), F32),
            pltpu.VMEM((groups - 1, owned, width), BF16),
            pltpu.VMEM((lons, n_attn, width), BF16),
            pltpu.VMEM((lons, n_mlp, width), BF16),
            pltpu.VMEM((lons, n_attn, width), BF16),
            pltpu.VMEM((lons, n_mlp, width), BF16),
            pltpu.VMEM((half, width), BF16),
            pltpu.VMEM((half, width), BF16),
            pltpu.VMEM((2, half, width), BF16),
            pltpu.VMEM((groups, 2, half, width), BF16),
            pltpu.SemaphoreType.DMA((pairs,)),
            pltpu.SemaphoreType.DMA((pairs,)),
            pltpu.SemaphoreType.DMA((4,)),
            pltpu.SemaphoreType.DMA((groups - 1,)),
            pltpu.SemaphoreType.DMA((groups - 1,)),
            pltpu.SemaphoreType.DMA((groups - 1,)),
            pltpu.SemaphoreType.DMA((groups - 1,)),
            pltpu.SemaphoreType.DMA((1,)),
            pltpu.SemaphoreType.DMA((1,)),
            pltpu.SemaphoreType.DMA((groups, 2)),
            pltpu.SemaphoreType.DMA((groups, 2)),
        ],
        compiler_params=pltpu.CompilerParams(
            collective_id=0, has_side_effects=True, vmem_limit_bytes=60 * 1024 * 1024
        ),
    )(
        patches.reshape(chans, count, width_p), embed_weight, channel_embed, agg_query.reshape(1, width),
        norm_gains, packed, decode_weight,
    )
    return out.reshape(chans, rows, cols, -1)


def solution(mesh):
    placed = (
        P("chan", None, "lon", None),
        P("chan", None, None),
        P("chan", None),
        P(),
        P(),
        P(None, None, "lon"),
        P(None, "lon", None),
        P(None, None, "lon"),
        P(None, "lon", None),
        P("chan", None, None),
    )
    return jax.shard_map(
        body, mesh=mesh, in_specs=placed, out_specs=P("chan", None, "lon", None), check_vma=False
    )
```

time: 301 us -> 54.9 us (0.18)
  blocking collectives: 252 us -> 0 us
  Pallas kernels: 0 us -> 50.9 us
  matrix products: 16.2 us -> 0 us
  starting transfers between devices: 11.7 us -> 0 us
  waiting for transfers between devices: 11 us -> 0 us
  other arithmetic: 4.94 us -> 0.77 us
    all_gather x9 -> x0, blocking collectives: 252 us -> none  [the longest x2 65.2 us: block_weights(): lax.all_gather(pieces[0], 'lon', axis=1, tiled=True)]
    pallas_call x0 -> x1, Pallas kernels: none -> 50.9 us  [body(): pl.pallas_call(functools.partial(kernel, groups, lons, inner, sizes), out...]
    dot_general x14 -> x0, matrix products: 15.6 us -> none  [the longest x1 2.99 us: body(): jnp.einsum('ct,cte->te', shares, embedded, precision=lax.Precision.HIGHEST)]
    all_to_all x3 -> x0, starting transfers between devices: 11 us -> none  [the longest x1 4.27 us: body(): lax.all_to_all(local_top, 'chan', split_axis=0, concat_axis=0, tiled=True)]
    ppermute x2 -> x0, waiting for transfers between devices: 6.41 us -> none  [from_behind(): return lax.ppermute(value, axis, pairs)]
    all_to_all x3 -> x0, waiting for transfers between devices: 4.6 us -> none  [the longest x1 4.59 us: body(): lax.all_to_all(numer, 'chan', split_axis=0, concat_axis=0, tiled=True)]
  transfers between devices with their start and end apart: 5 -> 0, of which waited for: 2 -> 0; matrix products, arithmetic and copies ran while one was open for 2% -> 0% of each run, Pallas kernels for 0% -> 0%
where the time goes in v1:
time: 54.9 us; the launch traced here: 54.7 us
  Pallas kernels  50.9 us (93%)
  local copies, waits for them, and re-layouts  2.93 us (5%)
  other arithmetic  0.77 us (1%)
    pallas_call x1, Pallas kernels, body(): pl.pallas_call(functools.partial(kernel, groups, lons, inner, sizes), out...  50.9 us
    unnamed x8, local copies, waits for them, and re-layouts  2.93 us

profile of v1, /device:TPU:0, one launch (start us, length us, event | category | flops | bytes accessed | tf_op | source)
XLA Modules:
  0.0 54.7 jit_solution(13071515181737167679)
XLA Ops:
  0.0 0.0 copy-start
  0.0 0.0 copy-start.1
  0.0 0.0 copy-start.2
  0.0 1.0 %copy.11 = bf16[2,256,128]{1,2,0:T(8,128)(2,1)S(1)} copy(bf16[2,256,128]{2,1,0:T(8,128)(2,1)} %param.17) | data formatting | bytes 262144 | tf_op args[7]
  1.1 0.0 copy-done
  1.1 0.0 copy-done.1
  1.1 0.0 copy-done.2
  1.1 0.8 %pad_maximum_fusion.packed = bf16[2,384,256]{2,1,0:T(8,128)(2,1)} fusion(bf16[2,128,256]{2,1,0:T(8,128)(2,1)S(1)} %copy-done, bf16[2,128,256]{2,1,0:T(8,128)(2,1)S(1)} %bitcast.6, bf16[2,32,256]{2,1,0:T(8,128)(2,1)S(1)} %copy-done.2, bf16[2,96,256]{2,1,0:T(8,128)(2,1)S(1)} %bitcast.8), kind=kLoop, calls=%fused_computation | loop fusion | flops 1572864 | bytes 786432 | tf_op jit(solution)/shard_map/concatenate | solution.py:402
  1.9 50.9 %shard_map.100 = bf16[8,256,128]{2,1,0:T(8,128)(2,1)} custom-call(bf16[8,256,128]{2,1,0:T(8,128)(2,1)} %bitcast.7, bf16[8,128,256]{2,1,0:T(8,128)(2,1)} %embed_weight.1, bf16[8,256]{1,0:T(8,128)(2,1)} %channel_embed.1, f32[1,256]{1,0:T(1,128)} %bitcast.9, f32[5,256]{1,0:T(8,128)} %gains.1, bf16[2,384,256]{2,1,0:T(8,128)(2,1)} %pad_maximum_fusion.packed, ...), custom_call_target="tpu_custom_call" | custom-call | tf_op jit(solution)/shard_map/pallas_call | solution.py:411
  52.8 1.9 %copy.13 = bf16[8,32,8,128]{3,2,1,0:T(8,128)(2,1)} copy(bf16[8,32,8,128]{3,2,1,0:T(8,128)(2,1)} %bitcast.5) | data formatting | bytes 1048576
Async XLA Ops:
  0.0 1.1 %copy-start = (bf16[2,128,256]{2,1,0:T(8,128)(2,1)S(1)}, bf16[2,128,256]{2,1,0:T(8,128)(2,1)}, u32[]{:S(2)}) copy-start(bf16[2,128,256]{2,1,0:T(8,128)(2,1)} %param.18) | copy-start | bytes 393220
  0.0 1.1 %copy-start.1 = (bf16[2,256,96]{1,2,0:T(8,128)(2,1)S(1)}, bf16[2,256,96]{1,2,0:T(8,128)(2,1)}, u32[]{:S(2)}) copy-start(bf16[2,256,96]{1,2,0:T(8,128)(2,1)} %param.15) | copy-start | bytes 294916
  0.0 1.1 %copy-start.2 = (bf16[2,32,256]{2,1,0:T(8,128)(2,1)S(1)}, bf16[2,32,256]{2,1,0:T(8,128)(2,1)}, u32[]{:S(2)}) copy-start(bf16[2,32,256]{2,1,0:T(8,128)(2,1)} %param.16) | copy-start | bytes 98308

commit v2 on v1

--- a/solution.py
+++ b/solution.py
@@ -199,10 +199,10 @@
 
 def kernel(
     groups, lons, inner, sizes,
-    patches, embed_weight, channel_embed, agg_query, gains, packed, decode_weight,
+    patches_hbm, embed_hbm, channel_embed, agg_query, gains, qkv_hbm, proj_hbm, up_hbm, down_hbm,
     out,
-    embedded, partial, aux_out, aux_in, mean_in, attn0, mlp0, attn1, mlp1, edge_out, edge_in, final_out, final_in,
-    chunk_send, chunk_recv, own_sem, agg_send, agg_recv, aux_send, aux_recv, edge_send, edge_recv, fin_send, fin_recv,
+    patches, embed_weight, up_in, embedded, partial, aux_out, aux_in, mean_in, attn0, mlp0, attn1, mlp1, edge_out, edge_in, final_out, final_in,
+    chunk_send, chunk_recv, own_sem, agg_send, agg_recv, aux_send, aux_recv, edge_send, edge_recv, fin_send, fin_recv, load_sem,
 ):
     chans, count, _ = patches.shape
     width = embed_weight.shape[2]
@@ -233,12 +233,53 @@
     }
     bufs = (attn0, mlp0, attn1, mlp1)
     own_copies = []
-    for at, buf in enumerate(bufs):
-        layer, rows = at // 2, pl.ds(0, n_attn) if at % 2 == 0 else pl.ds(n_attn, n_up + n_down)
-        copy = pltpu.make_async_copy(packed.at[layer, rows], buf.at[lon], own_sem.at[at])
+    for layer in range(2):
+        attn, mlp = bufs[2 * layer].at[lon], bufs[2 * layer + 1].at[lon]
+        moves = (
+            (up_hbm.at[layer], up_in.at[layer]),
+            (qkv_hbm.at[layer], attn.at[pl.ds(0, n_qkv)]),
+            (proj_hbm.at[layer], attn.at[pl.ds(n_qkv, n_proj)]),
+            (down_hbm.at[layer], mlp.at[pl.ds(n_up, n_down)]),
+        )
+        for at, (source, target) in enumerate(moves):
+            copy = pltpu.make_async_copy(source, target, own_sem.at[4 * layer + at])
+            copy.start()
+            own_copies.append(copy)
+    loads = [
+        pltpu.make_async_copy(patches_hbm, patches, load_sem.at[0]),
+        pltpu.make_async_copy(embed_hbm, embed_weight, load_sem.at[1]),
+    ]
+    for copy in loads:
         copy.start()
-        own_copies.append(copy)
-
+    for copy in own_copies:
+        copy.wait()
+    for layer in range(2):
+        bufs[2 * layer + 1][lon, :n_up] = up_in[layer].T
+    pl.semaphore_wait(barrier, greeted)
+
+    offset, gathers = 0, []
+    for at, order in enumerate((True, False, False, True)):
+        pairs = sem_count(outer, inner, order)
+        sends, recvs = Sems(chunk_send.at[pl.ds(offset, pairs)]), Sems(chunk_recv.at[pl.ds(offset, pairs)])
+        gathers.append(Gather(bufs[at], geometry, order, sends, recvs))
+        offset += pairs
+    flows = [one.steps() for one in gathers]
+
+    def advance(*which):
+        for i in which:
+            next(flows[i], None)
+
+    def drain(*which):
+        live = list(which)
+        while live:
+            for i in list(live):
+                if next(flows[i], "end") == "end":
+                    live.remove(i)
+
+    advance(0, 1)
+
+    for copy in loads:
+        copy.wait()
     query = agg_query[...]
     scores = []
     for c in range(chans):
@@ -246,20 +287,6 @@
         value = value + channel_embed[c : c + 1].astype(F32)
         embedded[c] = value
         scores.append(jnp.sum(value * query, axis=-1, keepdims=True) * width ** (-0.5))
-
-    for copy in own_copies:
-        copy.wait()
-    pl.semaphore_wait(barrier, greeted)
-
-    offset, gathers = 0, []
-    for at, order in enumerate((True, False, False, True)):
-        pairs = sem_count(outer, inner, order)
-        sends, recvs = Sems(chunk_send.at[pl.ds(offset, pairs)]), Sems(chunk_recv.at[pl.ds(offset, pairs)])
-        gathers.append(Gather(bufs[at], geometry, order, sends, recvs))
-        offset += pairs
-    flows = [one.steps() for one in gathers]
-    for flow in flows:
-        next(flow)
 
     top = functools.reduce(jnp.maximum, scores)
     shares = [jnp.exp(score - top) for score in scores]
@@ -296,13 +323,9 @@
     for copy in sent:
         copy.start()
 
-    def drain(*which):
-        live = [flows[i] for i in which]
-        while live:
-            for flow in list(live):
-                if next(flow, "end") == "end":
-                    live.remove(flow)
-
+    advance(0, 1, 2, 3)
+    for _ in range(4):
+        advance(0, 1, 2, 3)
     drain(0, 1)
 
     for copy in sent:
@@ -374,13 +397,8 @@
                     device_id=(source, west if part == 0 else lon) if step else (me, west), device_id_type=MESH,
                 ).wait_recv()
     back = order_matrix(True, BF16)
-    tokens = []
     for g in range(groups):
-        both = merged(final_in[g])
-        tokens.append(jnp.dot(back, both, preferred_element_type=F32).astype(BF16))
-    tokens = jnp.concatenate(tokens, axis=0)
-    for c in range(chans):
-        out[c] = jnp.dot(tokens, decode_weight[c], preferred_element_type=F32).astype(BF16)
+        out[g] = jnp.dot(back, merged(final_in[g]), preferred_element_type=F32).astype(BF16)
 
     for one in gathers:
         one.finish()
@@ -399,21 +417,22 @@
     owned = count // groups
     half = owned // 2
     assert cols == WC and owned <= 128
-    packed = jnp.concatenate(
-        [qkv_weight.transpose(0, 2, 1), proj_weight, up_weight.transpose(0, 2, 1), down_weight], axis=1
-    )
     sizes = (qkv_weight.shape[2], proj_weight.shape[1], up_weight.shape[2], down_weight.shape[1])
     n_attn, n_mlp = sizes[0] + sizes[1], sizes[2] + sizes[3]
     inner = inner_factor(lons)
     outer = lons // inner
     pairs = sum(sem_count(outer, inner, order) for order in (True, False, False, True))
     vmem = pl.BlockSpec(memory_space=pltpu.VMEM)
-    out = pl.pallas_call(
+    hbm = pl.BlockSpec(memory_space=pl.ANY)
+    tokens = pl.pallas_call(
         functools.partial(kernel, groups, lons, inner, sizes),
-        out_shape=jax.ShapeDtypeStruct((chans, count, decode_weight.shape[2]), BF16),
-        in_specs=[vmem] * 7,
+        out_shape=jax.ShapeDtypeStruct((groups, owned, width), BF16),
+        in_specs=[hbm] * 2 + [vmem] * 3 + [hbm] * 4,
         out_specs=vmem,
         scratch_shapes=[
+            pltpu.VMEM((chans, count, width_p), BF16),
+            pltpu.VMEM(embed_weight.shape, BF16),
+            pltpu.VMEM(up_weight.shape, BF16),
             pltpu.VMEM((chans, count, width), F32),
             pltpu.VMEM((groups, owned, width), BF16),
             pltpu.VMEM((groups, 8, 128), F32),
@@ -429,7 +448,7 @@
             pltpu.VMEM((groups, 2, half, width), BF16),
             pltpu.SemaphoreType.DMA((pairs,)),
             pltpu.SemaphoreType.DMA((pairs,)),
-            pltpu.SemaphoreType.DMA((4,)),
+            pltpu.SemaphoreType.DMA((8,)),
             pltpu.SemaphoreType.DMA((groups - 1,)),
             pltpu.SemaphoreType.DMA((groups - 1,)),
             pltpu.SemaphoreType.DMA((groups - 1,)),
@@ -438,15 +457,19 @@
             pltpu.SemaphoreType.DMA((1,)),
             pltpu.SemaphoreType.DMA((groups, 2)),
             pltpu.SemaphoreType.DMA((groups, 2)),
+            pltpu.SemaphoreType.DMA((2,)),
         ],
         compiler_params=pltpu.CompilerParams(
             collective_id=0, has_side_effects=True, vmem_limit_bytes=60 * 1024 * 1024
         ),
     )(
         patches.reshape(chans, count, width_p), embed_weight, channel_embed, agg_query.reshape(1, width),
-        norm_gains, packed, decode_weight,
+        norm_gains, qkv_weight.transpose(0, 2, 1), proj_weight, up_weight, down_weight,
     )
-    return out.reshape(chans, rows, cols, -1)
+    decoded = jnp.einsum(
+        "te,cep->ctp", tokens.reshape(count, width), decode_weight, preferred_element_type=F32
+    ).astype(BF16)
+    return decoded.reshape(chans, rows, cols, -1)
 
 
 def solution(mesh):

time: 54.9 us -> 48.8 us (0.89)
  Pallas kernels: 50.9 us -> 46.5 us
  local copies, waits for them, and re-layouts: 2.93 us -> 0.01 us
  matrix products: 0 us -> 2 us
  other arithmetic: 0.77 us -> 0 us
    pallas_call x1, Pallas kernels: 50.9 us -> 46.5 us  [body(): pl.pallas_call(functools.partial(kernel, groups, lons, inner, sizes), out...]
    unnamed x8 -> x2, local copies, waits for them, and re-layouts: 2.93 us -> 0.01 us
    dot_general x0 -> x1, matrix products: none -> 2 us  [body(): jnp.einsum('te,cep->ctp', tokens.reshape(count, width), decode_weight, pr...]
    concatenate x1 -> x0, other arithmetic: 0.77 us -> none  [body(): jnp.concatenate([qkv_weight.transpose(0, 2, 1), proj_weight, up_weight.tr...]
where the time goes in v2:
time: 48.8 us; the launch traced here: 48.5 us
  Pallas kernels  46.5 us (95%)
  matrix products  2 us (4%)
    pallas_call x1, Pallas kernels, body(): pl.pallas_call(functools.partial(kernel, groups, lons, inner, sizes), out...  46.5 us
    dot_general x1, matrix products, body(): jnp.einsum('te,cep->ctp', tokens.reshape(count, width), decode_weight, pr...  2 us

profile of v2, /device:TPU:0, one launch (start us, length us, event | category | flops | bytes accessed | tf_op | source)
XLA Modules:
  0.0 48.5 jit_solution(14155988432811369843)
XLA Ops:
  0.0 0.0 copy-start
  0.0 46.5 %shard_map.100 = bf16[4,64,256]{2,1,0:T(8,128)(2,1)} custom-call(bf16[8,256,128]{2,1,0:T(8,128)(2,1)} %bitcast.12, bf16[8,128,256]{2,1,0:T(8,128)(2,1)} %embed_hbm.1, bf16[8,256]{1,0:T(8,128)(2,1)} %channel_embed.1, f32[1,256]{1,0:T(1,128)} %bitcast.15, f32[5,256]{1,0:T(8,128)} %gains.1, bf16[2,96,256]{2,1,0:T(8,128)(2,1)} %bitcast.14, ...), custom_call_target="tpu_custom_call" | custom-call | tf_op jit(solution)/shard_map/pallas_call | solution.py:427
  46.5 0.0 copy-done
  46.5 2.0 %fusion = bf16[8,32,8,128]{3,2,1,0:T(8,128)(2,1)} fusion(bf16[256,256,1]{1,0,2:T(8,128)(2,1)} %bitcast.13, bf16[8,256,128]{2,1,0:T(8,128)(2,1)S(1)} %copy-done), kind=kOutput, calls=%fused_computation.1 | convolution fusion | flops 134479872 | bytes 1179648 | tf_op jit(solution)/shard_map/te,cep->ctp/dot_general | solution.py:469
Async XLA Ops:
  0.0 46.5 %copy-start = (bf16[8,256,128]{2,1,0:T(8,128)(2,1)S(1)}, bf16[8,256,128]{2,1,0:T(8,128)(2,1)}, u32[]{:S(2)}) copy-start(bf16[8,256,128]{2,1,0:T(8,128)(2,1)} %param.19) | copy-start | bytes 1572868

commit v3 on v2

--- a/solution.py
+++ b/solution.py
@@ -47,19 +47,14 @@
 
 
 class Gather:
-    def __init__(self, buf, geometry, x_first, sends, recvs):
-        self.buf = buf
-        self.geometry, self.x_first = geometry, x_first
+    def __init__(self, buf, geometry, parts, sends, recvs):
+        self.buf, self.geometry, self.parts = buf, geometry, parts
         self.sends, self.recvs = sends, recvs
-        self.pending = []
-        self.late = []
-
-    def rows(self, core):
-        half = self.buf.shape[1] // 2
-        return pl.ds(pl.multiple_of(core * half, half), half)
-
-    def copy(self, first, count, core, target, sem_pair):
-        piece = self.buf.at[pl.ds(first, count), self.rows(core)]
+        self.pending, self.late, self.inbox = [], [], []
+
+    def copy(self, shard, part, target, sem_pair):
+        size = self.buf.shape[1] // self.parts
+        piece = self.buf.at[shard, pl.ds(pl.multiple_of(part * size, size), size)]
         return pltpu.make_async_remote_copy(
             src_ref=piece,
             dst_ref=piece,
@@ -69,85 +64,90 @@
             device_id_type=MESH,
         )
 
-    def pair(self):
-        return self.sends.take(), self.recvs.take()
-
-    def begin(self, copy, when=None):
+    def begin(self, copy, when):
         if when is None:
             copy.start()
         else:
             pl.when(when)(copy.start)
         self.pending.append((copy, when))
 
-    def arrive(self, copy, when=None):
+    def arrive(self, copy, when):
         if when is None:
             copy.wait_recv()
         else:
             pl.when(when)(copy.wait_recv)
 
-    def share(self, first, count, when=None):
+    def exchange(self, shard, part, shard_in, part_in, peer, when, when_in, then):
+        pair = self.sends.take(), self.recvs.take()
+        self.begin(self.copy(shard, part, peer, pair), when)
+        arrival = self.copy(shard_in, part_in, peer, pair)
+        if then is None:
+            self.late.append((arrival, when_in))
+        else:
+            self.inbox.append((arrival, when_in, then))
+
+    def mine(self):
+        return self.geometry["part"](self.parts)
+
+    def to_core(self, shard, part, when):
         g = self.geometry
-        pair = self.pair()
-        self.begin(self.copy(first, count, g["core"], g["partner"], pair), when)
-        self.late.append((self.copy(first, count, 1 - g["core"], g["partner"], pair), when))
-
-    def across(self, z, when=None):
+        other = part + 1 - 2 * g["core"]
+        self.exchange(shard, part, shard, other, g["partner"], when, when, None)
+
+    def share(self, shard, when):
+        g, part = self.geometry, self.mine()
+        self.to_core(shard, part, when)
+        if self.parts == 4:
+            other = lax.rem(part + 2, 4)
+            self.exchange(
+                shard, part, shard, other, g["across"], when, when, lambda: self.to_core(shard, other, when)
+            )
+
+    def to_x(self, z, when):
         g = self.geometry
-        inner, x, core = g["inner"], g["x"], g["core"]
-        incoming = []
+        inner, x = g["inner"], g["x"]
         for step in range(1, inner):
-            pair = self.pair()
             to, source = lax.rem(x + step, inner), lax.rem(x + inner - step, inner)
-            peer = g["at"](g["z"], to)
-            self.begin(self.copy(z * inner + x, 1, core, peer, pair), when)
-            incoming.append((z * inner + source, self.copy(z * inner + source, 1, core, peer, pair), when))
-        return incoming
+            shard = z * inner + source
+            self.exchange(
+                z * inner + x, self.mine(), shard, self.mine(), g["at"](g["z"], to), when, when,
+                functools.partial(self.share, shard, when),
+            )
+
+    def to_z(self, step, way):
+        g = self.geometry
+        inner, outer, x, z = g["inner"], g["outer"], g["x"], g["z"]
+        if step >= outer - 1:
+            return
+        part = self.mine()
+
+        def inside(at):
+            return (at >= 0) & (at < outer), jnp.clip(at, 0, outer - 1)
+
+        has_next, after = inside(z + way)
+        has_out, out = inside(z - way * step)
+        has_in, source = inside(z - way * (step + 1))
+
+        def then():
+            self.to_z(step + 1, way)
+            self.to_x(source, has_in)
+            self.share(source * inner + x, has_in)
+
+        self.exchange(
+            out * inner + x, part, source * inner + x, part, g["at"](after, x), has_next & has_out, has_in, then
+        )
 
     def steps(self):
-        g = self.geometry
-        inner, outer, x, z, core = g["inner"], g["outer"], g["x"], g["z"], g["core"]
-        width = inner if self.x_first else 1
-
-        def first_of(at):
-            return at * inner if self.x_first else at * inner + x
-
-        if self.x_first:
-            incoming = self.across(z)
+        self.to_z(0, 1)
+        self.to_z(0, -1)
+        self.to_x(self.geometry["z"], None)
+        yield
+        while self.inbox:
+            now, self.inbox = self.inbox, []
+            for copy, when, then in now:
+                self.arrive(copy, when)
+                then()
             yield
-            for _, copy, when in incoming:
-                self.arrive(copy, when)
-            for shard, _, when in incoming:
-                self.share(shard, 1, when)
-        crossing = []
-        for step in range(outer):
-            if step < outer - 1:
-                right, left = self.pair(), self.pair()
-                here_right = (z + 1 < outer) & (z - step >= 0)
-                here_left = (z - 1 >= 0) & (z + step < outer)
-                at_right, at_left = jnp.maximum(z - step, 0), jnp.minimum(z + step, outer - 1)
-                up, down = jnp.minimum(z + 1, outer - 1), jnp.maximum(z - 1, 0)
-                self.begin(self.copy(first_of(at_right), width, core, g["at"](up, x), right), here_right)
-                self.begin(self.copy(first_of(at_left), width, core, g["at"](down, x), left), here_left)
-            if step == 0:
-                arrived = [(z, None)]
-            for at, when in arrived:
-                if not self.x_first:
-                    crossing += self.across(at, when)
-                if step:
-                    self.share(first_of(at), width, when)
-            if step == outer - 1:
-                break
-            yield
-            from_left, from_right = z - 1 - step >= 0, z + 1 + step < outer
-            at_left, at_right = jnp.maximum(z - 1 - step, 0), jnp.minimum(z + 1 + step, outer - 1)
-            self.arrive(self.copy(first_of(at_left), width, core, g["at"](down, x), right), from_left)
-            self.arrive(self.copy(first_of(at_right), width, core, g["at"](up, x), left), from_right)
-            arrived = [(at_left, from_left), (at_right, from_right)]
-        for shard, copy, when in crossing:
-            yield
-            self.arrive(copy, when)
-            self.share(shard, 1, when)
-        yield
         for copy, when in self.late:
             self.arrive(copy, when)
 
@@ -159,7 +159,13 @@
                 pl.when(when)(copy.wait_send)
 
 
-def window_block(state, gain_attn, gain_mlp, attn_ref, mlp_ref, sizes):
+def sem_count(outer, inner, parts):
+    lines = 2 * (outer - 1)
+    crosses = (1 + lines) * (inner - 1)
+    return lines + crosses + (lines + crosses) * (1 if parts == 2 else 3)
+
+
+def window_block(state, gain_attn, gain_mlp, attn_ref, mlp_ref, sizes, ready_mlp):
     n_qkv, n_up = sizes
     length, width = state.shape
     head_dim = width // HEADS
@@ -183,6 +189,7 @@
     w_proj = merged(attn_ref[:, n_qkv:])
     state = state + jnp.dot(mixed.astype(BF16), w_proj, preferred_element_type=F32)
     normed = layer_norm(state, gain_mlp).astype(BF16)
+    ready_mlp()
     w_up = merged(mlp_ref[:, :n_up])
     hidden = lax.dot_general(normed, w_up, NT, preferred_element_type=F32)
     hidden = jax.nn.gelu(hidden).astype(BF16)
@@ -190,11 +197,8 @@
     return state + jnp.dot(hidden, w_down, preferred_element_type=F32)
 
 
-def sem_count(outer, inner, x_first):
-    moves = 2 * (outer - 1)
-    if x_first:
-        return 2 * (inner - 1) + 2 * moves
-    return 2 * moves + (1 + moves) * (inner - 1) * 2
+def chunk_parts(groups):
+    return (2, 4, 2, 4) if groups % 4 == 0 else (2, 2, 2, 2)
 
 
 def kernel(
@@ -229,6 +233,8 @@
         "inner": inner, "outer": outer, "core": core,
         "x": lax.rem(lon, inner), "z": lon // inner,
         "partner": (me + 1 - 2 * core, lon),
+        "across": (me + 2 - 4 * (lax.rem(me, 4) // 2), lon),
+        "part": lambda parts: lax.rem(me, parts),
         "at": lambda z, x: (me, z * inner + x),
     }
     bufs = (attn0, mlp0, attn1, mlp1)
@@ -258,10 +264,10 @@
     pl.semaphore_wait(barrier, greeted)
 
     offset, gathers = 0, []
-    for at, order in enumerate((True, False, False, True)):
-        pairs = sem_count(outer, inner, order)
+    for at, parts in enumerate(chunk_parts(groups)):
+        pairs = sem_count(outer, inner, parts)
         sends, recvs = Sems(chunk_send.at[pl.ds(offset, pairs)]), Sems(chunk_recv.at[pl.ds(offset, pairs)])
-        gathers.append(Gather(bufs[at], geometry, order, sends, recvs))
+        gathers.append(Gather(bufs[at], geometry, parts, sends, recvs))
         offset += pairs
     flows = [one.steps() for one in gathers]
 
@@ -323,10 +329,13 @@
     for copy in sent:
         copy.start()
 
-    advance(0, 1, 2, 3)
-    for _ in range(4):
-        advance(0, 1, 2, 3)
-    drain(0, 1)
+    advance(0, 1)
+    advance(0, 1)
+    advance(2, 3)
+    advance(0, 1)
+    advance(0, 1)
+    advance(2, 3)
+    drain(0)
 
     for copy in sent:
         copy.wait_recv()
@@ -351,17 +360,19 @@
     def gain(i):
         return gains[i : i + 1]
 
-    state = window_block(state, gain(0), gain(1), attn0, mlp0, (n_qkv, n_up))
+    state = window_block(state, gain(0), gain(1), attn0, mlp0, (n_qkv, n_up), lambda: drain(1))
     edge_out[...] = state[:half].astype(BF16)
     edge = pltpu.make_async_remote_copy(
         src_ref=edge_out, dst_ref=edge_in, send_sem=edge_send.at[0], recv_sem=edge_recv.at[0],
         device_id=(me, west), device_id_type=MESH,
     )
     edge.start()
-    drain(2, 3)
+    for _ in range(4):
+        advance(2, 3)
+    drain(2)
     edge.wait_recv()
     moved = jnp.concatenate([state[half:], edge_in[...].astype(F32)], axis=0)
-    moved = window_block(moved, gain(2), gain(3), attn1, mlp1, (n_qkv, n_up))
+    moved = window_block(moved, gain(2), gain(3), attn1, mlp1, (n_qkv, n_up), lambda: drain(3))
     final = layer_norm(moved, gain(4)).astype(BF16)
     final_out[0] = final[half:]
     final_out[1] = final[:half]
@@ -421,7 +432,7 @@
     n_attn, n_mlp = sizes[0] + sizes[1], sizes[2] + sizes[3]
     inner = inner_factor(lons)
     outer = lons // inner
-    pairs = sum(sem_count(outer, inner, order) for order in (True, False, False, True))
+    pairs = sum(sem_count(outer, inner, parts) for parts in chunk_parts(groups))
     vmem = pl.BlockSpec(memory_space=pltpu.VMEM)
     hbm = pl.BlockSpec(memory_space=pl.ANY)
     tokens = pl.pallas_call(

time: 48.8 us -> 46.3 us (0.949)
  Pallas kernels: 46.5 us -> 44.1 us
    pallas_call x1, Pallas kernels: 46.5 us -> 44.1 us  [body(): pl.pallas_call(functools.partial(kernel, groups, lons, inner, sizes), out...]
where the time goes in v3:
time: 46.3 us; the launch traced here: 46.1 us
  Pallas kernels  44.1 us (95%)
  matrix products  2 us (4%)
    pallas_call x1, Pallas kernels, body(): pl.pallas_call(functools.partial(kernel, groups, lons, inner, sizes), out...  44.1 us
    dot_general x1, matrix products, body(): jnp.einsum('te,cep->ctp', tokens.reshape(count, width), decode_weight, pr...  2 us

profile of v3, /device:TPU:0, one launch (start us, length us, event | category | flops | bytes accessed | tf_op | source)
XLA Modules:
  0.0 46.1 jit_solution(695462941565530075)
XLA Ops:
  0.0 0.0 copy-start
  0.0 44.1 %shard_map.100 = bf16[4,64,256]{2,1,0:T(8,128)(2,1)} custom-call(bf16[8,256,128]{2,1,0:T(8,128)(2,1)} %bitcast.12, bf16[8,128,256]{2,1,0:T(8,128)(2,1)} %embed_hbm.1, bf16[8,256]{1,0:T(8,128)(2,1)} %channel_embed.1, f32[1,256]{1,0:T(1,128)} %bitcast.15, f32[5,256]{1,0:T(8,128)} %gains.1, bf16[2,96,256]{2,1,0:T(8,128)(2,1)} %bitcast.14, ...), custom_call_target="tpu_custom_call" | custom-call | tf_op jit(solution)/shard_map/pallas_call | solution.py:438
  44.1 0.0 copy-done
  44.1 2.0 %fusion = bf16[8,32,8,128]{3,2,1,0:T(8,128)(2,1)} fusion(bf16[256,256,1]{1,0,2:T(8,128)(2,1)} %bitcast.13, bf16[8,256,128]{2,1,0:T(8,128)(2,1)S(1)} %copy-done), kind=kOutput, calls=%fused_computation.1 | convolution fusion | flops 134479872 | bytes 1179648 | tf_op jit(solution)/shard_map/te,cep->ctp/dot_general | solution.py:480
Async XLA Ops:
  0.0 44.1 %copy-start = (bf16[8,256,128]{2,1,0:T(8,128)(2,1)S(1)}, bf16[8,256,128]{2,1,0:T(8,128)(2,1)}, u32[]{:S(2)}) copy-start(bf16[8,256,128]{2,1,0:T(8,128)(2,1)} %param.19) | copy-start | bytes 1572868

commit v4 on v3

--- a/solution.py
+++ b/solution.py
@@ -64,103 +64,75 @@
             device_id_type=MESH,
         )
 
-    def begin(self, copy, when):
-        if when is None:
-            copy.start()
-        else:
-            pl.when(when)(copy.start)
-        self.pending.append((copy, when))
-
-    def arrive(self, copy, when):
-        if when is None:
-            copy.wait_recv()
-        else:
-            pl.when(when)(copy.wait_recv)
-
-    def exchange(self, shard, part, shard_in, part_in, peer, when, when_in, then):
+    def exchange(self, shard, part, shard_in, part_in, peer, then):
         pair = self.sends.take(), self.recvs.take()
-        self.begin(self.copy(shard, part, peer, pair), when)
+        copy = self.copy(shard, part, peer, pair)
+        copy.start()
+        self.pending.append(copy)
         arrival = self.copy(shard_in, part_in, peer, pair)
         if then is None:
-            self.late.append((arrival, when_in))
+            self.late.append(arrival)
         else:
-            self.inbox.append((arrival, when_in, then))
+            self.inbox.append((arrival, then))
 
     def mine(self):
         return self.geometry["part"](self.parts)
 
-    def to_core(self, shard, part, when):
+    def to_core(self, shard, part):
         g = self.geometry
-        other = part + 1 - 2 * g["core"]
-        self.exchange(shard, part, shard, other, g["partner"], when, when, None)
-
-    def share(self, shard, when):
+        self.exchange(shard, part, shard, part + 1 - 2 * g["core"], g["partner"], None)
+
+    def share(self, shard):
         g, part = self.geometry, self.mine()
-        self.to_core(shard, part, when)
         if self.parts == 4:
             other = lax.rem(part + 2, 4)
-            self.exchange(
-                shard, part, shard, other, g["across"], when, when, lambda: self.to_core(shard, other, when)
-            )
-
-    def to_x(self, z, when):
+            self.exchange(shard, part, shard, other, g["across"], lambda: self.to_core(shard, other))
+        self.to_core(shard, part)
+
+    def to_x(self, z):
         g = self.geometry
         inner, x = g["inner"], g["x"]
         for step in range(1, inner):
             to, source = lax.rem(x + step, inner), lax.rem(x + inner - step, inner)
             shard = z * inner + source
             self.exchange(
-                z * inner + x, self.mine(), shard, self.mine(), g["at"](g["z"], to), when, when,
-                functools.partial(self.share, shard, when),
+                z * inner + x, self.mine(), shard, self.mine(), g["at"](g["z"], to),
+                functools.partial(self.share, shard),
             )
 
-    def to_z(self, step, way):
+    def to_z(self):
         g = self.geometry
         inner, outer, x, z = g["inner"], g["outer"], g["x"], g["z"]
-        if step >= outer - 1:
-            return
-        part = self.mine()
-
-        def inside(at):
-            return (at >= 0) & (at < outer), jnp.clip(at, 0, outer - 1)
-
-        has_next, after = inside(z + way)
-        has_out, out = inside(z - way * step)
-        has_in, source = inside(z - way * (step + 1))
-
-        def then():
-            self.to_z(step + 1, way)
-            self.to_x(source, has_in)
-            self.share(source * inner + x, has_in)
-
-        self.exchange(
-            out * inner + x, part, source * inner + x, part, g["at"](after, x), has_next & has_out, has_in, then
-        )
+        for step in range(1, outer):
+            to, source = lax.rem(z + step, outer), lax.rem(z + outer - step, outer)
+            shard = source * inner + x
+
+            def then(source=source, shard=shard):
+                self.to_x(source)
+                self.share(shard)
+
+            self.exchange(z * inner + x, self.mine(), shard, self.mine(), g["at"](to, x), then)
 
     def steps(self):
-        self.to_z(0, 1)
-        self.to_z(0, -1)
-        self.to_x(self.geometry["z"], None)
+        self.to_z()
+        self.to_x(self.geometry["z"])
         yield
         while self.inbox:
             now, self.inbox = self.inbox, []
-            for copy, when, then in now:
-                self.arrive(copy, when)
+            for copy, then in now:
+                copy.wait_recv()
                 then()
             yield
-        for copy, when in self.late:
-            self.arrive(copy, when)
+        for copy in self.late:
+            copy.wait_recv()
 
     def finish(self):
-        for copy, when in self.pending:
-            if when is None:
-                copy.wait_send()
-            else:
-                pl.when(when)(copy.wait_send)
+        for copy in self.pending:
+            copy.wait_send()
 
 
 def sem_count(outer, inner, parts):
-    lines = 2 * (outer - 1)
+    lines = outer - 1
     crosses = (1 + lines) * (inner - 1)
     return lines + crosses + (lines + crosses) * (1 if parts == 2 else 3)
 
@@ -330,11 +302,10 @@
         copy.start()
 
     advance(0, 1)
+    advance(2, 3)
     advance(0, 1)
     advance(2, 3)
-    advance(0, 1)
-    advance(0, 1)
-    advance(2, 3)
+    advance(1)
     drain(0)
 
     for copy in sent:
@@ -367,8 +338,8 @@
         device_id=(me, west), device_id_type=MESH,
     )
     edge.start()
-    for _ in range(4):
-        advance(2, 3)
+    advance(2, 3)
+    advance(3)
     drain(2)
     edge.wait_recv()
     moved = jnp.concatenate([state[half:], edge_in[...].astype(F32)], axis=0)

time: 46.3 us -> 39.7 us (0.86)
  Pallas kernels: 44.1 us -> 37.5 us
    pallas_call x1, Pallas kernels: 44.1 us -> 37.5 us  [body(): pl.pallas_call(functools.partial(kernel, groups, lons, inner, sizes), out...]
where the time goes in v4:
time: 39.7 us; the launch traced here: 39.5 us
  Pallas kernels  37.5 us (94%)
  matrix products  2 us (5%)
    pallas_call x1, Pallas kernels, body(): pl.pallas_call(functools.partial(kernel, groups, lons, inner, sizes), out...  37.5 us
    dot_general x1, matrix products, body(): jnp.einsum('te,cep->ctp', tokens.reshape(count, width), decode_weight, pr...  2 us

profile of v4, /device:TPU:0, one launch (start us, length us, event | category | flops | bytes accessed | tf_op | source)
XLA Modules:
  0.0 39.5 jit_solution(8540481982814978798)
XLA Ops:
  0.0 0.0 copy-start
  0.0 37.5 %shard_map.100 = bf16[4,64,256]{2,1,0:T(8,128)(2,1)} custom-call(bf16[8,256,128]{2,1,0:T(8,128)(2,1)} %bitcast.12, bf16[8,128,256]{2,1,0:T(8,128)(2,1)} %embed_hbm.1, bf16[8,256]{1,0:T(8,128)(2,1)} %channel_embed.1, f32[1,256]{1,0:T(1,128)} %bitcast.15, f32[5,256]{1,0:T(8,128)} %gains.1, bf16[2,96,256]{2,1,0:T(8,128)(2,1)} %bitcast.14, ...), custom_call_target="tpu_custom_call" | custom-call | tf_op jit(solution)/shard_map/pallas_call | solution.py:409
  37.5 0.0 copy-done
  37.5 2.0 %fusion = bf16[8,32,8,128]{3,2,1,0:T(8,128)(2,1)} fusion(bf16[256,256,1]{1,0,2:T(8,128)(2,1)} %bitcast.13, bf16[8,256,128]{2,1,0:T(8,128)(2,1)S(1)} %copy-done), kind=kOutput, calls=%fused_computation.1 | convolution fusion | flops 134479872 | bytes 1179648 | tf_op jit(solution)/shard_map/te,cep->ctp/dot_general | solution.py:451
Async XLA Ops:
  0.0 37.5 %copy-start = (bf16[8,256,128]{2,1,0:T(8,128)(2,1)S(1)}, bf16[8,256,128]{2,1,0:T(8,128)(2,1)}, u32[]{:S(2)}) copy-start(bf16[8,256,128]{2,1,0:T(8,128)(2,1)} %param.19) | copy-start | bytes 1572868
